TPU v7x, 256 devices: a whole 4x4x8 slice. The times are simulated.
256 devices in a mesh: wide: 128 (over y, z, x), cols: 2 (over core).
Axes of the slice: x: 4, y: 4, z: 8, core: 2. Of those that a mesh axis runs over, the one named last changes fastest.
Arguments:
- factor: float32 [262144, 256], P('wide', 'cols')
- gates: float32 [8, 128, 128], replicated, may hold values from -0.5 to 0.5
- gate_layout: int32 [2048], P('wide'), may hold values from 0 to 7
- jump_masks: int32 [3], replicated, may hold values from 1 to 127
- jump_rates: float32 [3], replicated, may hold values from 0.1 to 0.4
- sketch_perm: int32 [1024], replicated, may hold values from 0 to 1023, each once
- bases: float32 [8, 64, 64], replicated, may hold values from -0.75 to 0.75
- basis_index: int32 [128, 32], P('wide'), may hold values from 0 to 7
Outputs:
- new_factor: float32 [262144, 256], P('wide', 'cols')
- weights: float32 [128, 2048], P('wide', 'cols')
Inputs may be any that keep to these rules, and one draw needn't show every extreme that they name: `jump_masks`: nonzero bit masks over the high qubits. `sketch_perm`: each value appears once.
All inputs are finite; a program needn't handle non-finite values.
Results may differ from a plain program's by a relative error of at most 0.0003.
Values sent between devices are 32-bit elements; how exact they have to be, the bound alone decides.
No kernel may reach another device: no remote copies, remote signals or barrier semaphores. Data moves between devices by JAX's collectives and lax.ppermute only.
A program may use at most 64 MiB of HBM per device.

v0:
```python
import jax
import jax.numpy as jnp
from jax import lax
from jax.sharding import PartitionSpec as P

NS_ITERS = 7
HIGH = lax.Precision.HIGHEST


def apply_blocks(mats, index, data):
    chosen = jnp.take(mats, index, axis=0)
    return jnp.einsum("bij,bjc->bic", chosen, data, precision=HIGH)


def flip_rows(data, mask, count):
    shaped = data.reshape(count, data.shape[0] // count, data.shape[1])
    source = jnp.bitwise_xor(jnp.arange(count, dtype=jnp.int32), mask)
    return jnp.take(shaped, source, axis=0).reshape(data.shape)


def sketch_table(sketch_perm, rank):
    target = sketch_perm % rank
    sign = 1.0 - 2.0 * (sketch_perm // rank % 2).astype(jnp.float32)
    hit = target[:, None] == jnp.arange(rank, dtype=jnp.int32)[None, :]
    return jnp.where(hit, sign[:, None], jnp.zeros((), jnp.float32))


def mixed_stack(source, table, first, coefs, masks, count):
    rank = table.shape[1]
    width = source.shape[1]
    sources = []
    blocks = []
    for k in range(len(coefs)):
        flipped = source if k == 0 else flip_rows(source, masks[k - 1], count)
        sources.append(coefs[k] * flipped)
        blocks.append(lax.dynamic_slice_in_dim(table, k * rank + first, width, 0))
    joined = jnp.concatenate(sources, axis=1)
    table_rows = jnp.concatenate(blocks, axis=0)
    return jnp.dot(joined, table_rows, precision=HIGH, preferred_element_type=jnp.float32)


def newton_root(mat, eye, iters):
    fro = jnp.sqrt(jnp.sum(mat * mat))
    approx = mat / (fro + 1e-06)
    inverse = eye
    for step in range(iters):
        middle = 1.5 * eye - 0.5 * jnp.dot(inverse, approx, precision=HIGH)
        approx = jnp.dot(approx, middle, precision=HIGH)
        inverse = jnp.dot(middle, inverse, precision=HIGH)
    return (approx, inverse, fro)


def per_device(factor, gates, gate_layout, jump_masks, jump_rates, sketch_perm, bases, basis_index):
    rows, width = factor.shape
    order = gates.shape[1]
    count = lax.axis_size("wide")
    halves = lax.axis_size("cols")
    column_index = lax.axis_index("cols")
    rank = width * halves
    jumps = jump_rates.shape[0]
    gated = apply_blocks(gates, gate_layout, factor.reshape(rows // order, order, width)).reshape(
        rows, width
    )
    moved = lax.all_to_all(gated, "wide", split_axis=0, concat_axis=0, tiled=True)
    keep = 1.0 - 0.5 * jnp.sum(jump_rates)
    coefs = [keep] + [jnp.sqrt(jump_rates[k]) for k in range(jumps)]
    table = sketch_table(sketch_perm, rank)
    first = column_index * width
    terms = mixed_stack(moved, table, first, coefs, jump_masks, count)
    sketch_own = lax.psum_scatter(terms, "cols", scatter_dimension=1, tiled=True)
    sketch = lax.all_gather(sketch_own, "cols", axis=1, tiled=True)
    share = rows // halves
    mine = lax.dynamic_slice_in_dim(sketch, column_index * share, share, 0)
    gram_part = lax.dot_general(
        mine, mine, (((0,), (0,)), ((), ())), precision=HIGH, preferred_element_type=jnp.float32
    )
    gram = lax.psum(gram_part, ("wide", "cols"))
    eye = jnp.eye(rank, dtype=jnp.float32)
    unused, inverse, fro = newton_root(gram, eye, NS_ITERS)
    parts = []
    for k in range(jumps + 1):
        right = moved if k == 0 else flip_rows(moved, jump_masks[k - 1], count)
        parts.append(
            coefs[k]
            * lax.dot_general(
                sketch,
                right,
                (((0,), (0,)), ((), ())),
                precision=HIGH,
                preferred_element_type=jnp.float32,
            )
        )
    proj_own = jnp.concatenate(parts, axis=1)
    proj_sum = lax.psum(proj_own, "wide")
    coeff = lax.dot_general(
        inverse,
        proj_sum,
        (((0,), (0,)), ((), ())),
        precision=HIGH,
        preferred_element_type=jnp.float32,
    )
    core_part = lax.dot_general(
        coeff, coeff, (((1,), (1,)), ((), ())), precision=HIGH, preferred_element_type=jnp.float32
    )
    core = lax.psum(core_part, "cols")
    approx_two, unused_two, fro_two = newton_root(core, eye, NS_ITERS)
    root_own = jnp.sqrt(fro_two + 1e-06) * lax.dynamic_slice_in_dim(approx_two, first, width, 1)
    mixing_own = jnp.dot(inverse, root_own, precision=HIGH)
    new_own = jnp.dot(sketch, mixing_own, precision=HIGH)
    rot = bases.shape[1]
    rotated = apply_blocks(bases, basis_index.reshape(-1), new_own.reshape(rows // rot, rot, width))
    partial_value = (jnp.sum(rotated * rotated, axis=2) / rank).reshape(1, rows)
    weights = lax.psum_scatter(partial_value, "cols", scatter_dimension=1, tiled=True)
    return (new_own, weights)


def solution(mesh):
    return jax.shard_map(
        per_device,
        mesh=mesh,
        in_specs=(P("wide", "cols"), P(), P("wide"), P(), P(), P(), P(), P("wide", None)),
        out_specs=(P("wide", "cols"), P("wide", "cols")),
        check_vma=False,
    )
```

profile of v0, /device:TPU:1, one launch (start us, length us, event | category | flops | bytes accessed | tf_op | source)
XLA Modules:
  0.0 657.7 jit_solution(18310592391966807667)
XLA Ops:
  7.2 0.7 compare_select_fusion.5
  8.6 1.7 gather_fusion
  10.3 2.2 fusion.12
  12.5 16.3 %all-to-all-start = ((f32[128,16,128]{2,1,0:T(8,128)}), f32[128,16,128]{2,1,0:T(8,128)S(1)}, u32[]{:S(2)}, u32[]{:S(2)}) async-start(f32[128,16,128]{2,1,0:T(8,128)} %bitcast.1), calls=%async_computation | async-start | bytes 2097152 | tf_op jit(solution)/shard_map/all_to_all | solution.py:64
  34.3 1.2 compare_and_fusion.2
  35.5 1.3 compare_select_fusion
  36.7 1.8 compare_and_fusion
  39.6 16.5 %all-to-all-done = f32[128,16,128]{2,1,0:T(8,128)S(1)} async-done(((f32[128,16,128]{2,1,0:T(8,128)}), f32[128,16,128]{2,1,0:T(8,128)S(1)}, u32[]{:S(2)}, u32[]{:S(2)}) %all-to-all-start) | async-done | bytes 1048608 | tf_op jit(solution)/shard_map/all_to_all | solution.py:64
  56.1 0.8 gather_fusion.3
  56.8 0.9 broadcast_select_fusion.1
  57.7 1.0 copy-done.4
  58.7 1.0 broadcast_multiply_fusion.1
  59.7 0.8 gather_fusion.4
  60.7 1.0 copy-done.5
  61.7 1.0 broadcast_multiply_fusion
  62.7 0.8 gather_fusion.2
  63.9 0.8 copy-done.7
  65.7 4.9 fusion
  70.6 13.1 %reduce-scatter.5.cloned.1.call-done = f32[2048,128]{1,0:T(8,128)} async-done(((f32[2048,256]{1,0:T(8,128)}), f32[2048,128]{1,0:T(8,128)}) %reduce-scatter.5.cloned.1.call-update) | async-done | bytes 1048592 | tf_op jit(solution)/shard_map/reduce_scatter | solution.py:70
  83.8 19.0 %all-gather.2.cloned.1.call-done = f32[2048,256]{1,0:T(8,128)} async-done(((f32[2048,128]{1,0:T(8,128)}), f32[2048,256]{1,0:T(8,128)}) %all-gather.2.cloned.1.call-update) | async-done | bytes 2097168 | tf_op jit(solution)/shard_map/all_gather | solution.py:71
  102.7 4.1 fusion.10
  107.4 5.4 convolution_multiply_fusion.16
  112.8 3.4 convolution_multiply_fusion.15
  116.3 3.4 convolution_multiply_fusion.17
  119.7 3.6 convolution_multiply_fusion.18
  123.3 0.8 pad_maximum_fusion
  124.2 234.4 %all-reduce.4.cloned.1.call-done = f32[256,256]{1,0:T(8,128)} async-done(((f32[256,256]{1,0:T(8,128)}), f32[256,256]{1,0:T(8,128)}) %all-reduce.4.cloned.1.call-update) | async-done | bytes 262160 | tf_op jit(solution)/shard_map/psum | solution.py:77
  358.6 1.6 multiply_reduce_fusion.1
  360.9 1.3 select_subtract_fusion.13
  362.5 1.3 fusion.31
  370.0 1.1 fusion.58
  371.1 206.0 %all-reduce.6.cloned.1.call-done = f32[256,512]{1,0:T(8,128)} async-done(((f32[256,512]{1,0:T(8,128)}), f32[256,512]{1,0:T(8,128)}) %all-reduce.6.cloned.1.call-update) | async-done | bytes 524304 | tf_op jit(solution)/shard_map/psum | solution.py:94
  577.2 1.7 fusion.59
  578.9 1.3 fusion.60
  580.6 1.6 gather_fusion.1
  582.2 30.0 %all-reduce.8.cloned.1.call-done = f32[256,256]{1,0:T(8,128)} async-done(((f32[256,256]{1,0:T(8,128)}), f32[256,256]{1,0:T(8,128)}) %all-reduce.8.cloned.1.call-update) | async-done | bytes 262160 | tf_op jit(solution)/shard_map/psum | solution.py:105
  612.2 1.6 multiply_reduce_fusion
  614.5 1.3 select_subtract_fusion.6
  616.0 1.3 fusion.32
  622.4 1.1 fusion.70
  623.9 1.3 select_subtract_fusion
  625.7 1.4 fusion.28
  627.1 1.8 fusion.72
  629.0 1.0 copy-done.9
  629.9 1.5 fusion.8
  631.5 2.0 div.43
  633.5 15.3 %reduce-scatter.7.cloned.1.call-done = f32[1024,1]{1,0:T(8,128)} async-done(((f32[2048,1]{1,0:T(8,128)}), f32[1024,1]{1,0:T(8,128)}) %reduce-scatter.7.cloned.1.call-update) | async-done | bytes 4112
  648.8 1.8 copy.11
  (101 shorter events, 19.3 us)
Async XLA Ops:
  7.2 3.1 copy-start
  10.3 18.6 %copy-start.16 = (f32[3]{0:T(128)S(1)}, f32[3]{0:T(128)}, u32[]{:S(2)}) copy-start(f32[3]{0:T(128)} %param.14) | copy-start | bytes 40
  10.3 22.6 %copy-start.17 = (s32[3]{0:T(128)S(1)}, s32[3]{0:T(128)}, u32[]{:S(2)}) copy-start(s32[3]{0:T(128)} %param.13) | copy-start | bytes 40
  10.3 28.2 %copy-start.15 = (s32[1024]{0:T(1024)S(1)}, s32[1024]{0:T(1024)}, u32[]{:S(2)}) copy-start(s32[1024]{0:T(1024)} %param.15) | copy-start | bytes 12292
  12.5 43.6 %all-to-all-start = ((f32[128,16,128]{2,1,0:T(8,128)}), f32[128,16,128]{2,1,0:T(8,128)S(1)}, u32[]{:S(2)}, u32[]{:S(2)}) async-start(f32[128,16,128]{2,1,0:T(8,128)} %bitcast.1), calls=%async_computation | async-start | bytes 2097152 | tf_op jit(solution)/shard_map/all_to_all | solution.py:64
  28.8 54.8 %reduce-scatter.5.cloned.1.call-start = ((), (), s32[]{:S(2)}) async-start(), calls=%async_computation.3 | async-start | bytes 3145728 | tf_op jit(solution)/shard_map/reduce_scatter | solution.py:70
  56.1 7.7 %copy-start.2 = (f32[128,16,128]{2,1,0:T(8,128)}, f32[128,16,128]{2,1,0:T(8,128)S(1)}, u32[]{:S(2)}) copy-start(f32[128,16,128]{2,1,0:T(8,128)S(1)} %all-to-all-done) | copy-start | bytes 3145732
  57.7 1.0 copy-start.4
  60.7 1.0 copy-start.5
  61.7 1.8 copy-start.18
  63.7 1.0 copy-start.7
  63.7 1.6 copy-start.12
  63.8 1.9 copy-start.13
  63.8 1.9 copy-start.14
  70.5 13.2 %copy-start.19 = (s32[1,32]{1,0:T(1,128)S(1)}, s32[1,32]{1,0:T(1,128)}, u32[]{:S(2)}) copy-start(s32[1,32]{1,0:T(1,128)} %param.17) | copy-start | bytes 388
  70.6 32.2 %all-gather.2.cloned.1.call-start = ((), (), s32[]{:S(2)}) async-start(), calls=%async_computation.4 | async-start | bytes 3145728 | tf_op jit(solution)/shard_map/all_gather | solution.py:71
  83.7 274.9 %all-reduce.4.cloned.1.call-start = ((), (), s32[]{:S(2)}) async-start(), calls=%async_computation.5 | async-start | bytes 524288 | tf_op jit(solution)/shard_map/psum | solution.py:77
  106.9 5.9 copy-start.1
  106.9 470.3 %all-reduce.6.cloned.1.call-start = ((), (), s32[]{:S(2)}) async-start(), calls=%async_computation.6 | async-start | bytes 1048576 | tf_op jit(solution)/shard_map/psum | solution.py:94
  107.4 5.4 copy-start.6
  112.8 3.5 copy-start.8
  116.3 3.5 copy-start.3
  124.2 488.0 %all-reduce.8.cloned.1.call-start = ((), (), s32[]{:S(2)}) async-start(), calls=%async_computation.7 | async-start | bytes 524288 | tf_op jit(solution)/shard_map/psum | solution.py:105
  369.6 210.9 %copy-start.11 = (f32[8,64,64]{2,1,0:T(8,128)S(1)}, f32[8,64,64]{2,1,0:T(8,128)}, u32[]{:S(2)}) copy-start(f32[8,64,64]{2,1,0:T(8,128)} %param.16) | copy-start | bytes 393220
  580.3 68.5 %reduce-scatter.7.cloned.1.call-start = ((), (), s32[]{:S(2)}) async-start(), calls=%async_computation.8 | async-start | bytes 1572864
  625.7 4.3 copy-start.10
  629.0 1.0 copy-start.9
Sparse Core Ops, SparseCore 0:
  70.7 12.9 reduce-scatter.4
  85.6 17.0 all-gather.1
  109.1 249.4 all-reduce.3
  365.3 211.7 all-reduce.5
  580.4 31.7 all-reduce.7
  633.6 15.1 reduce-scatter.6
where the time goes:
time: 666 us; the launch traced here: 658 us
  waiting for transfers between devices  534 us (80%)
  matrix products  55.9 us (8%)
  between operations  19.3 us (3%)
  starting transfers between devices  17.3 us (3%)
  local copies, waits for them, and re-layouts  16.1 us (2%)
  other arithmetic  14.9 us (2%)
    psum x1, waiting for transfers between devices, per_device(): gram = lax.psum(gram_part, ('wide', 'cols'))  234 us
    psum x1, waiting for transfers between devices, per_device(): proj_sum = lax.psum(proj_own, 'wide')  206 us
    psum x1, waiting for transfers between devices, per_device(): core = lax.psum(core_part, 'cols')  30 us
    all_gather x1, waiting for transfers between devices, per_device(): sketch = lax.all_gather(sketch_own, 'cols', axis=1, tiled=True)  19 us
    all_to_all x1, waiting for transfers between devices, per_device(): lax.all_to_all(gated, 'wide', split_axis=0, concat_axis=0, tiled=True)  16.5 us
    all_to_all x1, starting transfers between devices, per_device(): lax.all_to_all(gated, 'wide', split_axis=0, concat_axis=0, tiled=True)  16.3 us
    dot_general x4, matrix products, per_device(): lax.dot_general(sketch, right, (((0,), (0,)), ((), ())), precision=HIGH,...  15.9 us
    unnamed x7, waiting for transfers between devices  15.4 us
  transfers between devices with their start and end apart: 7, of which 7 were waited for; matrix products, arithmetic and copies ran while one was open for 6% of the time, Pallas kernels for 0%

commit v1 on v0

--- a/solution.py
+++ b/solution.py
@@ -74,7 +74,8 @@
     gram_part = lax.dot_general(
         mine, mine, (((0,), (0,)), ((), ())), precision=HIGH, preferred_element_type=jnp.float32
     )
-    gram = lax.psum(gram_part, ("wide", "cols"))
+    inner = lax.psum(gram_part, "wide")
+    gram = lax.psum(inner, "cols")
     eye = jnp.eye(rank, dtype=jnp.float32)
     unused, inverse, fro = newton_root(gram, eye, NS_ITERS)
     parts = []

time: 666 us -> 471 us (0.71)
  waiting for transfers between devices: 534 us -> 342 us
    psum x2, waiting for transfers between devices: 440 us -> 250 us  [the longest x1 216 us: per_device(): inner = lax.psum(gram_part, 'wide')]
  transfers between devices with their start and end apart: 7 -> 7, of which waited for: 7 -> 7; matrix products, arithmetic and copies ran while one was open for 6% -> 2% of each run, Pallas kernels for 0% -> 0%
where the time goes in v1:
time: 471 us; the launch traced here: 464 us
  waiting for transfers between devices  342 us (73%)
  matrix products  53.8 us (11%)
  between operations  19.2 us (4%)
  starting transfers between devices  17.3 us (4%)
  local copies, waits for them, and re-layouts  16.8 us (4%)
  other arithmetic  14.8 us (3%)
    psum x1, waiting for transfers between devices, per_device(): inner = lax.psum(gram_part, 'wide')  216 us
    psum x1, waiting for transfers between devices, per_device(): gram = lax.psum(inner, 'cols')  33.9 us
    psum x1, waiting for transfers between devices, per_device(): core = lax.psum(core_part, 'cols')  28.6 us
    all_gather x1, waiting for transfers between devices, per_device(): sketch = lax.all_gather(sketch_own, 'cols', axis=1, tiled=True)  18.5 us
    dot_general x4, matrix products, per_device(): lax.dot_general(sketch, right, (((0,), (0,)), ((), ())), precision=HIGH,...  17.2 us
    all_to_all x1, waiting for transfers between devices, per_device(): lax.all_to_all(gated, 'wide', split_axis=0, concat_axis=0, tiled=True)  16.6 us
    all_to_all x1, starting transfers between devices, per_device(): lax.all_to_all(gated, 'wide', split_axis=0, concat_axis=0, tiled=True)  16.3 us
    unnamed x7, waiting for transfers between devices  15.4 us
  transfers between devices with their start and end apart: 7, of which 7 were waited for; matrix products, arithmetic and copies ran while one was open for 2% of the time, Pallas kernels for 0%

profile of v1, /device:TPU:1, one launch (start us, length us, event | category | flops | bytes accessed | tf_op | source)
XLA Modules:
  0.0 463.6 jit_solution(2797367765873250057)
XLA Ops:
  7.2 0.7 compare_select_fusion.5
  8.6 1.7 gather_fusion
  10.3 2.2 fusion.12
  12.5 16.3 %all-to-all-start = ((f32[128,16,128]{2,1,0:T(8,128)}), f32[128,16,128]{2,1,0:T(8,128)S(1)}, u32[]{:S(2)}, u32[]{:S(2)}) async-start(f32[128,16,128]{2,1,0:T(8,128)} %bitcast.1), calls=%async_computation | async-start | bytes 2097152 | tf_op jit(solution)/shard_map/all_to_all | solution.py:64
  34.2 1.2 compare_and_fusion.2
  35.3 1.3 compare_select_fusion
  36.6 1.8 compare_and_fusion
  38.8 0.7 constant_dynamic-slice_fusion.3
  39.5 16.6 %all-to-all-done = f32[128,16,128]{2,1,0:T(8,128)S(1)} async-done(((f32[128,16,128]{2,1,0:T(8,128)}), f32[128,16,128]{2,1,0:T(8,128)S(1)}, u32[]{:S(2)}, u32[]{:S(2)}) %all-to-all-start) | async-done | bytes 1048608 | tf_op jit(solution)/shard_map/all_to_all | solution.py:64
  56.1 0.8 gather_fusion.3
  56.8 0.9 broadcast_select_fusion.1
  57.7 1.0 copy-done.3
  58.7 1.1 broadcast_multiply_fusion.1
  59.8 0.8 gather_fusion.4
  60.7 1.0 copy-done.5
  61.7 1.0 broadcast_multiply_fusion
  62.8 0.8 gather_fusion.2
  63.9 0.8 copy-done.7
  65.7 4.9 %fusion = f32[2048,256]{1,0:T(8,128)} fusion(f32[2048,128]{1,0:T(8,128)S(1)} %copy-done.13, f32[2048,128]{1,0:T(8,128)S(1)} %copy-done.12, f32[2048,128]{1,0:T(8,128)S(1)} %get-tuple-element.19, f32[2048,128]{1,0:T(8,128)S(1)} %get-tuple-element.20, f32[128,256]{1,0:T(8,128)S(1)} %get-tuple-element.6, f32[128,256]{1,0:T(8,128)S(1)} %get-tuple-element.7, ...), kind=kOutput, calls=%fused_computation.5 | convolution fusion | flops 3224764416 | bytes 6815744 | tf_op jit(solution)/shard_map/dot_general | solution.py:39
  70.6 13.1 %reduce-scatter.5.cloned.1.call-done = f32[2048,128]{1,0:T(8,128)} async-done(((f32[2048,256]{1,0:T(8,128)}), f32[2048,128]{1,0:T(8,128)}) %reduce-scatter.5.cloned.1.call-update) | async-done | bytes 1048592 | tf_op jit(solution)/shard_map/reduce_scatter | solution.py:70
  84.2 18.5 %all-gather.2.cloned.1.call-done = f32[2048,256]{1,0:T(8,128)} async-done(((f32[2048,128]{1,0:T(8,128)}), f32[2048,256]{1,0:T(8,128)}) %all-gather.2.cloned.1.call-update) | async-done | bytes 2097168 | tf_op jit(solution)/shard_map/all_gather | solution.py:71
  102.7 5.4 %convolution_multiply_fusion.18 = f32[256,128]{1,0:T(8,128)S(1)} fusion(f32[2048,256]{1,0:T(8,128)} %all-gather.2.cloned.1.call-done, f32[2048,128]{1,0:T(8,128)} %bitcast.115, f32[]{:T(128)S(6)} %sub.57), kind=kOutput, calls=%fused_computation.46 | convolution fusion | flops 805339136 | bytes 3276804 | tf_op jit(solution)/shard_map/dot_general | solution.py:86
  108.2 4.7 %convolution_multiply_fusion.17 = f32[256,128]{1,0:T(8,128)S(1)} fusion(f32[2048,256]{1,0:T(8,128)S(1)} %copy-done.1, f32[2048,128]{1,0:T(8,128)} %bitcast.118, f32[]{:T(128)} %bitcast.3), kind=kOutput, calls=%fused_computation.45 | convolution fusion | flops 805339136 | bytes 3276804 | tf_op jit(solution)/shard_map/dot_general | solution.py:86
  112.9 3.4 convolution_multiply_fusion.16
  116.4 3.6 convolution_multiply_fusion.15
  120.0 0.8 pad_maximum_fusion
  120.8 2.5 fusion.10
  123.5 215.6 %all-reduce.9.cloned.1.call-done = (f32[256,256]{1,0:T(8,128)}, f32[256,512]{1,0:T(8,128)}) async-done(((f32[256,256]{1,0:T(8,128)}, f32[256,512]{1,0:T(8,128)}), (f32[256,256]{1,0:T(8,128)}, f32[256,512]{1,0:T(8,128)})) %all-reduce.9.cloned.1.call-update) | async-done | bytes 786448 | tf_op jit(solution)/shard_map/psum | solution.py:77
  339.1 33.9 %all-reduce.5.cloned.1.call-done = f32[256,256]{1,0:T(8,128)} async-done(((f32[256,256]{1,0:T(8,128)}), f32[256,256]{1,0:T(8,128)}) %all-reduce.5.cloned.1.call-update) | async-done | bytes 262160 | tf_op jit(solution)/shard_map/psum | solution.py:78
  373.1 1.6 multiply_reduce_fusion.1
  375.4 1.3 select_subtract_fusion.13
  376.9 1.3 fusion.31
  384.9 0.7 copy-done.11
  386.2 1.3 fusion.60
  387.9 1.6 gather_fusion.1
  389.5 28.6 %all-reduce.7.cloned.1.call-done = f32[256,256]{1,0:T(8,128)} async-done(((f32[256,256]{1,0:T(8,128)}), f32[256,256]{1,0:T(8,128)}) %all-reduce.7.cloned.1.call-update) | async-done | bytes 262160 | tf_op jit(solution)/shard_map/psum | solution.py:106
  418.1 1.6 multiply_reduce_fusion
  420.4 1.3 select_subtract_fusion.6
  421.9 1.3 fusion.32
  428.3 1.1 fusion.70
  429.8 1.3 select_subtract_fusion
  431.6 1.4 fusion.28
  433.0 1.9 fusion.72
  434.9 1.0 copy-done.8
  435.8 1.5 fusion.8
  437.4 2.0 div.43
  439.4 15.3 %reduce-scatter.7.cloned.1.call-done = f32[1024,1]{1,0:T(8,128)} async-done(((f32[2048,1]{1,0:T(8,128)}), f32[1024,1]{1,0:T(8,128)}) %reduce-scatter.7.cloned.1.call-update) | async-done | bytes 4112
  454.7 1.8 copy.11
  (103 shorter events, 19.6 us)
Async XLA Ops:
  7.2 3.1 copy-start
  10.3 18.6 %copy-start.17 = (f32[3]{0:T(128)S(1)}, f32[3]{0:T(128)}, u32[]{:S(2)}) copy-start(f32[3]{0:T(128)} %param.14) | copy-start | bytes 40
  10.3 22.6 %copy-start.18 = (s32[3]{0:T(128)S(1)}, s32[3]{0:T(128)}, u32[]{:S(2)}) copy-start(s32[3]{0:T(128)} %param.13) | copy-start | bytes 40
  10.3 28.1 %copy-start.16 = (s32[1024]{0:T(1024)S(1)}, s32[1024]{0:T(1024)}, u32[]{:S(2)}) copy-start(s32[1024]{0:T(1024)} %param.15) | copy-start | bytes 12292
  12.5 43.6 %all-to-all-start = ((f32[128,16,128]{2,1,0:T(8,128)}), f32[128,16,128]{2,1,0:T(8,128)S(1)}, u32[]{:S(2)}, u32[]{:S(2)}) async-start(f32[128,16,128]{2,1,0:T(8,128)} %bitcast.1), calls=%async_computation | async-start | bytes 2097152 | tf_op jit(solution)/shard_map/all_to_all | solution.py:64
  28.8 54.8 %reduce-scatter.5.cloned.1.call-start = ((), (), s32[]{:S(2)}) async-start(), calls=%async_computation.3 | async-start | bytes 3145728 | tf_op jit(solution)/shard_map/reduce_scatter | solution.py:70
  56.1 7.7 %copy-start.2 = (f32[128,16,128]{2,1,0:T(8,128)}, f32[128,16,128]{2,1,0:T(8,128)S(1)}, u32[]{:S(2)}) copy-start(f32[128,16,128]{2,1,0:T(8,128)S(1)} %all-to-all-done) | copy-start | bytes 3145732
  57.7 1.0 copy-start.3
  60.7 1.0 copy-start.5
  61.7 1.8 copy-start.19
  63.7 1.0 copy-start.7
  63.8 1.6 copy-start.12
  63.8 1.9 copy-start.13
  63.8 1.9 copy-start.15
  70.6 32.2 %all-gather.2.cloned.1.call-start = ((), (), s32[]{:S(2)}) async-start(), calls=%async_computation.4 | async-start | bytes 3145728 | tf_op jit(solution)/shard_map/all_gather | solution.py:71
  83.7 255.3 %all-reduce.9.cloned.1.call-start = ((), (), s32[]{:S(2)}) async-start(), calls=%async_computation.8 | async-start | bytes 1572864 | tf_op jit(solution)/shard_map/psum | solution.py:77
  102.7 5.4 %copy-start.1 = (f32[2048,256]{1,0:T(8,128)S(1)}, f32[2048,256]{1,0:T(8,128)}, u32[]{:S(2)}) copy-start(f32[2048,256]{1,0:T(8,128)} %all-gather.2.cloned.1.call-done) | copy-start | bytes 6291460
  108.2 4.8 %copy-start.4 = (f32[128,16,128]{2,1,0:T(8,128)S(1)}, f32[128,16,128]{2,1,0:T(8,128)}, u32[]{:S(2)}) copy-start(f32[128,16,128]{2,1,0:T(8,128)} %copy-done.3) | copy-start | bytes 3145732
  112.9 3.5 copy-start.6
  120.0 219.1 %copy-start.20 = (s32[1,32]{1,0:T(1,128)S(1)}, s32[1,32]{1,0:T(1,128)}, u32[]{:S(2)}) copy-start(s32[1,32]{1,0:T(1,128)} %param.17) | copy-start | bytes 388
  123.4 249.7 %all-reduce.5.cloned.1.call-start = ((), (), s32[]{:S(2)}) async-start(), calls=%async_computation.5 | async-start | bytes 524288 | tf_op jit(solution)/shard_map/psum | solution.py:78
  339.0 79.0 %all-reduce.7.cloned.1.call-start = ((), (), s32[]{:S(2)}) async-start(), calls=%async_computation.6 | async-start | bytes 524288 | tf_op jit(solution)/shard_map/psum | solution.py:106
  382.9 2.7 copy-start.14
  384.1 3.8 copy-start.10
  384.9 0.7 copy-start.11
  387.6 67.1 %reduce-scatter.7.cloned.1.call-start = ((), (), s32[]{:S(2)}) async-start(), calls=%async_computation.7 | async-start | bytes 1572864
  431.6 4.3 copy-start.9
  434.9 1.0 copy-start.8
Sparse Core Ops, SparseCore 0:
  70.7 12.9 reduce-scatter.4
  85.6 17.0 all-gather.1
  123.5 215.4 all-reduce.8
  341.5 31.5 all-reduce.4
  387.7 30.3 all-reduce.6
  439.5 15.1 reduce-scatter.6
